TPU v7x, 32 devices: a whole 2x2x4 slice. The times are simulated.
32 devices in a mesh: grp: 4 (over y, x), sub: 8 (over z, core).
Axes of the slice: x: 2, y: 2, z: 4, core: 2. Of those that a mesh axis runs over, the one named last changes fastest.
Arguments:
- right_side: float32 [24576, 160], P(('grp', 'sub')), may hold values from -6 to 6
- iterate_in: float32 [24576, 160], P(('grp', 'sub')), may hold values from -6 to 6
- diagonal: float32 [24576], P(('grp', 'sub')), may hold values from 1.5 to 4
- block_values: bfloat16 [32, 6, 3, 128, 128], P(('grp', 'sub')), may hold values from -0.125 to 0.125
- block_cols: int32 [32, 6, 3], P(('grp', 'sub')), may hold values from 0 to 5, as said below
- couple_left: bfloat16 [24576, 128], P(('grp', 'sub')), may hold values from -0.125 to 0.125
- couple_right: bfloat16 [24576, 128], P(('grp', 'sub')), may hold values from -0.125 to 0.125
- send_rows: int32 [32, 2, 128], P(('grp', 'sub')), may hold values from 0 to 767, as said below
- local_inverse: bfloat16 [32, 1024, 1024], P(('grp', 'sub')), may hold values from -0.3 to 2.3, as said below
- coarse_basis: bfloat16 [32, 1024, 32], P(('grp', 'sub')), may hold values from -0.1875 to 0.1875
- coarse_diag: float32 [32, 32, 32], P(('grp', 'sub')), may hold values from -54 to 59.5, as said below
- coarse_up: float32 [32, 32, 32], P(('grp', 'sub')), may hold values from -29.7 to 27
Outputs:
- iterate: float32 [24576, 160], P(('grp', 'sub'))
- residual: float32 [24576, 160], P(('grp', 'sub'))
Inputs may be any that keep to these rules, and one draw needn't show every extreme that they name: `block_cols`: the 3 column blocks of one row block are distinct. `send_rows`: the 256 rows listed for one subdomain are distinct. `local_inverse`: each block is symmetric positive definite. `coarse_diag`: each block is symmetric; with coarse_up the coarse operator is symmetric positive definite.
All inputs are finite; a program needn't handle non-finite values.
Results may differ from a plain program's by a relative error of at most 0.0032.
Values may be sent and summed in bfloat16 or wider, within the bound.
No kernel may reach another device: no remote copies, remote signals or barrier semaphores. Data moves between devices by JAX's collectives and lax.ppermute only.
A program may use at most 64 MiB of HBM per device.

v0:
```python
import jax
import jax.numpy as jnp
from jax import lax
from jax.sharding import PartitionSpec as P


def with_halo(cells, sides, width):
    for axis, dim in sides:
        count = lax.axis_size(axis)
        ends = count - 1
        head = lax.slice_in_dim(cells, 0, width, axis=dim)
        tail = lax.slice_in_dim(cells, cells.shape[dim] - width, cells.shape[dim], axis=dim)
        cells = jnp.concatenate(
            [
                lax.ppermute(tail, axis, [(i, (i + 1) % count) for i in range(ends)]),
                cells,
                lax.ppermute(head, axis, [((i + 1) % count, i) for i in range(ends)]),
            ],
            axis=dim,
        )
    return cells


def chol_solve(factor, values):
    halfway = lax.linalg.triangular_solve(factor, values, left_side=True, lower=True)
    return lax.linalg.triangular_solve(
        factor, halfway, left_side=True, lower=True, transpose_a=True
    )


def solve_chain(diagonal_blocks, upper, values):
    highest = lax.Precision.HIGHEST
    blocks_total = diagonal_blocks.shape[0]
    padded_total = 1
    while padded_total < blocks_total:
        padded_total = padded_total * 2
    extra = padded_total - blocks_total
    block_width = diagonal_blocks.shape[1]
    identity = jnp.eye(block_width, dtype=jnp.float32)
    diag_now = jnp.concatenate(
        [diagonal_blocks, jnp.broadcast_to(identity, (extra, block_width, block_width))], axis=0
    )
    upper_now = jnp.concatenate(
        [upper[:-1], jnp.zeros((extra + 1, block_width, block_width), jnp.float32)], axis=0
    )
    rhs_now = jnp.concatenate([values, jnp.zeros((extra,) + values.shape[1:], jnp.float32)], axis=0)
    levels = []
    while diag_now.shape[0] > 1:
        diag_even = diag_now[0::2]
        diag_odd = diag_now[1::2]
        upper_even = upper_now[0::2]
        upper_odd = upper_now[1::2]
        rhs_even = rhs_now[0::2]
        rhs_odd = rhs_now[1::2]
        factor = jnp.linalg.cholesky(diag_odd)
        stacked = jnp.concatenate([jnp.swapaxes(upper_even, 1, 2), upper_odd, rhs_odd], axis=2)
        through = chol_solve(factor, stacked)
        toward_left = through[:, :, :block_width]
        toward_right = through[:, :, block_width : 2 * block_width]
        odd_loads = through[:, :, 2 * block_width :]
        new_diag = diag_even - jnp.einsum(
            "mab,mbc->mac", upper_even, toward_left, precision=highest
        )
        new_upper = -jnp.einsum("mab,mbc->mac", upper_even, toward_right, precision=highest)
        new_rhs = rhs_even - jnp.einsum("mab,mbn->man", upper_even, odd_loads, precision=highest)
        from_diag = jnp.einsum("mba,mbc->mac", upper_odd, toward_right, precision=highest)
        from_rhs = jnp.einsum("mba,mbn->man", upper_odd, odd_loads, precision=highest)
        new_diag = new_diag - jnp.concatenate(
            [jnp.zeros_like(from_diag[:1]), from_diag[:-1]], axis=0
        )
        new_rhs = new_rhs - jnp.concatenate([jnp.zeros_like(from_rhs[:1]), from_rhs[:-1]], axis=0)
        levels.append((toward_left, toward_right, odd_loads))
        diag_now, upper_now, rhs_now = (new_diag, new_upper, new_rhs)
    solution = chol_solve(jnp.linalg.cholesky(diag_now[0]), rhs_now[0])[None]
    for toward_left, toward_right, odd_loads in reversed(levels):
        next_sol = jnp.concatenate([solution[1:], jnp.zeros_like(solution[:1])], axis=0)
        odd_part = (
            odd_loads
            - jnp.einsum("mab,mbn->man", toward_left, solution, precision=highest)
            - jnp.einsum("mab,mbn->man", toward_right, next_sol, precision=highest)
        )
        solution = jnp.stack([solution, odd_part], axis=1).reshape((-1,) + solution.shape[1:])
    return solution[:blocks_total]


def shards(
    right_side,
    iterate_in,
    diagonal,
    block_values,
    block_cols,
    couple_left,
    couple_right,
    send_rows,
    local_inverse,
    coarse_basis,
    coarse_diag,
    coarse_up,
):
    bf16 = jnp.bfloat16
    f32 = jnp.float32
    highest = lax.Precision.HIGHEST
    intersection = send_rows.shape[2]
    rows_own = right_side.shape[0]
    cases = right_side.shape[1]
    row_blocks = block_cols.shape[1]
    modes = coarse_basis.shape[2]
    column_blocks = block_cols[0]
    sent_left_rows = send_rows[0, 0]
    sent_right_rows = send_rows[0, 1]

    def neighbour_rows(source):
        boundary = jnp.stack([source[sent_left_rows], source[sent_right_rows]])
        padded = with_halo(boundary, ((("grp", "sub"), 0),), 1)
        return (padded[0], padded[3])

    def apply_operator(vector):
        rounded = vector.astype(bf16)
        from_left, from_right = neighbour_rows(rounded)
        blocks = rounded.reshape(row_blocks, -1, cases)
        picked = blocks[column_blocks]
        sparse = jnp.einsum(
            "itab,itbn->ian", block_values[0], picked, preferred_element_type=f32
        ).reshape(rows_own, cases)
        coupled = jnp.dot(couple_left, from_left, preferred_element_type=f32) + jnp.dot(
            couple_right, from_right, preferred_element_type=f32
        )
        return diagonal[:, None] * vector + (sparse + coupled)

    residual_start = right_side - apply_operator(iterate_in)
    rounded = residual_start.astype(bf16)
    from_left, from_right = neighbour_rows(rounded)
    extended = jnp.concatenate([from_left, rounded, from_right], axis=0)
    local_part = jnp.dot(local_inverse[0], extended, preferred_element_type=f32)
    coarse_in = jnp.dot(coarse_basis[0].T, extended, preferred_element_type=f32)
    blocks_diag = lax.all_gather(coarse_diag, "sub", axis=0, tiled=True)
    blocks_up = lax.all_gather(coarse_up, "sub", axis=0, tiled=True)
    group = lax.axis_index("grp")
    groups = lax.axis_size("grp")
    member = lax.axis_index("sub")
    members = lax.axis_size("sub")
    keep = (group < groups - 1).astype(f32)
    first_up = blocks_up[0]
    last_up = blocks_up[members - 1] * keep
    columns = lax.all_gather(coarse_in[None], "sub", axis=0, tiled=True)
    width = columns.shape[2]
    inner_count = members - 1
    empty_cols = jnp.zeros((inner_count, modes, modes), f32)
    left_cols = empty_cols.at[0].set(first_up.T)
    right_cols = empty_cols.at[inner_count - 1].set(last_up)
    stacked = jnp.concatenate([columns[1:], left_cols, right_cols], axis=2)
    solved = solve_chain(blocks_diag[1:], blocks_up[1:], stacked)
    sol_loads = solved[:, :, :width]
    sol_left = solved[:, :, width : width + modes]
    sol_right = solved[:, :, width + modes :]
    self_left = jnp.dot(first_up, sol_left[0], precision=highest)
    cross_term = jnp.dot(first_up, sol_right[0], precision=highest)
    rhs_first = jnp.dot(first_up, sol_loads[0], precision=highest)
    self_right = jnp.dot(last_up.T, sol_right[-1], precision=highest)
    rhs_last = jnp.dot(last_up.T, sol_loads[-1], precision=highest)
    sep_diag = lax.all_gather(blocks_diag[0][None], "grp", axis=0, tiled=True)
    sep_rhs = lax.all_gather(columns[0][None], "grp", axis=0, tiled=True)
    all_left = lax.all_gather(self_left[None], "grp", axis=0, tiled=True)
    all_right = lax.all_gather(self_right[None], "grp", axis=0, tiled=True)
    all_cross = lax.all_gather(cross_term[None], "grp", axis=0, tiled=True)
    all_first = lax.all_gather(rhs_first[None], "grp", axis=0, tiled=True)
    all_last = lax.all_gather(rhs_last[None], "grp", axis=0, tiled=True)
    prev_right = jnp.concatenate([jnp.zeros_like(all_right[:1]), all_right[:-1]], axis=0)
    prev_last = jnp.concatenate([jnp.zeros_like(all_last[:1]), all_last[:-1]], axis=0)
    reduced_diag = sep_diag - all_left - prev_right
    reduced_rhs = sep_rhs - all_first - prev_last
    sep_sol = solve_chain(reduced_diag, -all_cross, reduced_rhs)
    padded_sol = jnp.concatenate([sep_sol, jnp.zeros_like(sep_sol[:1])], axis=0)
    mine = lax.dynamic_index_in_dim(padded_sol, group, 0, keepdims=False)
    after = lax.dynamic_index_in_dim(padded_sol, group + 1, 0, keepdims=False)
    inner_sol = (
        sol_loads
        - jnp.einsum("ivw,wn->ivn", sol_left, mine, precision=highest)
        - jnp.einsum("ivw,wn->ivn", sol_right, after, precision=highest)
    )
    group_sol = jnp.concatenate([mine[None], inner_sol], axis=0)
    coarse_sol = lax.dynamic_index_in_dim(group_sol, member, 0, keepdims=False)
    correction = local_part + jnp.dot(
        coarse_basis[0], coarse_sol.astype(bf16), preferred_element_type=f32
    )
    tails = jnp.stack([correction[:intersection], correction[intersection + rows_own :]])
    returned = with_halo(tails.astype(jnp.bfloat16), ((("grp", "sub"), 0),), 1).astype(tails.dtype)
    owned = correction[intersection : intersection + rows_own]
    owned = owned.at[sent_right_rows].add(returned[3])
    owned = owned.at[sent_left_rows].add(returned[0])
    inner = lax.psum(jnp.sum(residual_start * owned, axis=0), ("grp", "sub"))
    image = apply_operator(owned)
    curvature = lax.psum(jnp.sum(owned * image, axis=0), ("grp", "sub"))
    step_size = inner / curvature
    return (iterate_in + step_size * owned, residual_start - step_size * image)


def solution(mesh):
    in_specs = (
        P(("grp", "sub"), None),
        P(("grp", "sub"), None),
        P(("grp", "sub")),
        P(("grp", "sub"), None, None, None, None),
        P(("grp", "sub"), None, None),
        P(("grp", "sub"), None),
        P(("grp", "sub"), None),
        P(("grp", "sub"), None, None),
        P(("grp", "sub"), None, None),
        P(("grp", "sub"), None, None),
        P(("grp", "sub"), None, None),
        P(("grp", "sub"), None, None),
    )
    out_specs = (P(("grp", "sub"), None), P(("grp", "sub"), None))
    return jax.shard_map(shards, mesh=mesh, in_specs=in_specs, out_specs=out_specs, check_vma=False)
```

profile of v0, /device:TPU:14, one launch (start us, length us, event | category | flops | bytes accessed | tf_op | source)
XLA Modules:
  0.0 289.2 jit_solution(11546375033526299166)
XLA Ops:
  0.7 1.3 copy.175
  2.0 0.8 fusion.182
  2.8 1.5 gather_fusion.2
  4.3 1.9 collective-permute-start.1
  6.2 1.5 gather_fusion.1
  7.7 2.4 collective-permute-start
  10.4 14.8 %all_gather.32 = f32[8,32,32]{2,1,0:T(8,128)S(1)} all-gather(f32[1,32,32]{2,1,0:T(8,128)S(1)} %copy-done.34), channel_id=1, replica_groups=mesh['grp'=4,'sub'=8] {'sub'}, dimensions={0}, use_global_device_ids=true | all-gather | bytes 36864 | tf_op jit(solution)/shard_map/all_gather | solution.py:137
  25.2 14.0 %all_gather.30 = f32[8,32,32]{2,1,0:T(8,128)S(1)} all-gather(f32[1,32,32]{2,1,0:T(8,128)S(1)} %copy-done.35), channel_id=1, replica_groups=mesh['grp'=4,'sub'=8] {'sub'}, dimensions={0}, use_global_device_ids=true | all-gather | bytes 36864 | tf_op jit(solution)/shard_map/all_gather | solution.py:136
  39.5 11.7 %custom-call.47 = f32[4,32,32]{2,1,0:T(8,128)S(1)} custom-call(f32[4,32,32]{2,1,0:T(8,128)S(1)} %copy.185), custom_call_target="Cholesky" | custom-call | tf_op jit(solution)/shard_map/jit(cholesky)/cholesky | solution.py:55
  51.3 0.6 compare_reduce_fusion.6
  51.9 1.7 gather_fusion
  53.8 1.9 convolution_bitcast_fusion.1
  55.7 0.7 select_bitcast_fusion
  56.4 1.1 fusion.73
  57.5 1.9 fusion.211
  59.6 1.1 gather_fusion.4
  60.7 1.0 gather_fusion.3
  61.8 4.0 %collective-permute-start.3 = (bf16[1,128,160]{1,2,0:T(8,128)(2,1)S(1)}, bf16[1,128,160]{1,2,0:T(8,128)(2,1)S(1)}, u32[]{:S(2)}, u32[]{:S(2)}) collective-permute-start(bf16[1,128,160]{1,2,0:T(8,128)(2,1)S(1)} %bitcast.412), channel_id=1, source_target_pairs={{1,0},{2,1},{3,2},{4,3},{5,4},{6,5},{7,6},{8,7},{9,8},{10,9},{11,1... | collective-permute-start | bytes 122888 | tf_op jit(solution)/shard_map/ppermute | solution.py:17
  65.9 1.9 collective-permute-start.2
  68.0 0.7 copy.187
  68.7 11.2 %custom-call.48 = f32[4,1,32,32]{2,3,1,0:T(8,128)} custom-call(f32[4,1,32,32]{3,2,1,0:T(8,128)} %select_bitcast_fusion), custom_call_target="InvertDiagBlocksLowerTriangular" | custom-call | tf_op jit(solution)/shard_map/triangular_solve | solution.py:26
  79.9 9.1 %all_gather.31 = f32[4,32,32]{2,1,0:T(8,128)S(1)} all-gather(f32[1,32,32]{2,1,0:T(8,128)S(1)} %slice-done.1), channel_id=1, replica_groups=mesh['grp'=4,'sub'=8] {'grp'}, dimensions={0}, use_global_device_ids=true | all-gather | bytes 20480 | tf_op jit(solution)/shard_map/all_gather | solution.py:161
  89.0 0.7 copy.210
  90.5 12.7 %all-gather = f32[256,160]{1,0:T(8,128)S(1)} all-gather(f32[32,160]{1,0:T(8,128)S(1)} %convolution_bitcast_fusion.11), channel_id=2, replica_groups=mesh['grp'=4,'sub'=8] {'sub'}, dimensions={0}, use_global_device_ids=true | all-gather | bytes 184320 | tf_op jit(solution)/shard_map/all_gather | solution.py:145
  106.0 5.9 %custom-call.57 = f32[2,32,32]{2,1,0:T(8,128)S(1)} custom-call(f32[2,32,32]{2,1,0:T(8,128)S(1)} %fusion.117), custom_call_target="Cholesky" | custom-call | tf_op jit(solution)/shard_map/jit(cholesky)/cholesky | solution.py:55
  112.1 4.9 %custom-call.49 = f32[2,1,32,32]{2,3,1,0:T(8,128)S(1)} custom-call(f32[2,1,32,32]{3,2,1,0:T(8,128)S(1)} %fusion.119), custom_call_target="InvertDiagBlocksLowerTriangular" | custom-call | tf_op jit(solution)/shard_map/triangular_solve | solution.py:26
  119.1 2.9 %custom-call.58 = f32[1,32,32]{2,1,0:T(8,128)S(1)} custom-call(f32[1,32,32]{2,1,0:T(8,128)S(1)} %fusion.169), custom_call_target="Cholesky" | custom-call | tf_op jit(solution)/shard_map/jit(cholesky)/cholesky | solution.py:55
  123.2 2.4 custom-call.50
  126.9 2.9 %cholesky.184 = f32[32,32]{1,0:T(8,128)S(1)} custom-call(f32[32,32]{1,0:T(8,128)S(1)} %fusion.150), custom_call_target="Cholesky" | custom-call | tf_op jit(solution)/shard_map/jit(cholesky)/cholesky | solution.py:74
  129.9 0.6 compare_reduce_fusion.3
  131.1 2.4 custom-call.51
  136.5 7.0 %all-gather.6 = f32[128,160]{1,0:T(8,128)S(1)} all-gather(f32[32,160]{1,0:T(8,128)S(1)} %slice-done), channel_id=8, replica_groups=mesh['grp'=4,'sub'=8] {'grp'}, dimensions={0}, use_global_device_ids=true | all-gather | bytes 102400 | tf_op jit(solution)/shard_map/all_gather | solution.py:162
  143.4 8.9 %all-gather.4 = f32[128,160]{1,0:T(8,128)S(1)} all-gather(f32[32,160]{1,0:T(8,128)S(1)} %convolution_bitcast_fusion.7), channel_id=6, replica_groups=mesh['grp'=4,'sub'=8] {'grp'}, dimensions={0}, use_global_device_ids=true | all-gather | bytes 102400 | tf_op jit(solution)/shard_map/all_gather | solution.py:166
  152.4 7.1 %all-gather.5 = f32[128,160]{1,0:T(8,128)S(1)} all-gather(f32[32,160]{1,0:T(8,128)S(1)} %fusion.101), channel_id=7, replica_groups=mesh['grp'=4,'sub'=8] {'grp'}, dimensions={0}, use_global_device_ids=true | all-gather | bytes 102400 | tf_op jit(solution)/shard_map/all_gather | solution.py:167
  159.6 8.7 %all-gather.3 = f32[128,32]{1,0:T(8,128)S(1)} all-gather(f32[32,32]{1,0:T(8,128)S(1)} %copy.214), channel_id=5, replica_groups=mesh['grp'=4,'sub'=8] {'grp'}, dimensions={0}, use_global_device_ids=true | all-gather | bytes 20480 | tf_op jit(solution)/shard_map/all_gather | solution.py:165
  168.5 6.7 %all-gather.2 = f32[128,32]{1,0:T(8,128)S(1)} all-gather(f32[32,32]{1,0:T(8,128)S(1)} %fusion.145), channel_id=4, replica_groups=mesh['grp'=4,'sub'=8] {'grp'}, dimensions={0}, use_global_device_ids=true | all-gather | bytes 20480 | tf_op jit(solution)/shard_map/all_gather | solution.py:164
  175.4 8.9 %all-gather.1 = f32[128,32]{1,0:T(8,128)S(1)} all-gather(f32[32,32]{1,0:T(8,128)S(1)} %copy.208), channel_id=3, replica_groups=mesh['grp'=4,'sub'=8] {'grp'}, dimensions={0}, use_global_device_ids=true | all-gather | bytes 20480 | tf_op jit(solution)/shard_map/all_gather | solution.py:163
  184.6 5.9 %custom-call.59 = f32[2,32,32]{2,1,0:T(8,128)S(1)} custom-call(f32[2,32,32]{2,1,0:T(8,128)S(1)} %fusion.112), custom_call_target="Cholesky" | custom-call | tf_op jit(solution)/shard_map/jit(cholesky)/cholesky | solution.py:55
  190.7 4.9 %custom-call.52 = f32[2,1,32,32]{2,3,1,0:T(8,128)S(1)} custom-call(f32[2,1,32,32]{3,2,1,0:T(8,128)S(1)} %fusion.118), custom_call_target="InvertDiagBlocksLowerTriangular" | custom-call | tf_op jit(solution)/shard_map/triangular_solve | solution.py:26
  197.6 2.9 %custom-call.60 = f32[1,32,32]{2,1,0:T(8,128)S(1)} custom-call(f32[1,32,32]{2,1,0:T(8,128)S(1)} %fusion.158), custom_call_target="Cholesky" | custom-call | tf_op jit(solution)/shard_map/jit(cholesky)/cholesky | solution.py:55
  200.6 0.6 compare_reduce_fusion.1
  201.2 0.7 fusion.143
  201.9 2.4 custom-call.53
  205.5 2.9 %cholesky.216 = f32[32,32]{1,0:T(8,128)S(1)} custom-call(f32[32,32]{1,0:T(8,128)S(1)} %fusion.149), custom_call_target="Cholesky" | custom-call | tf_op jit(solution)/shard_map/jit(cholesky)/cholesky | solution.py:74
  208.5 0.6 compare_reduce_fusion
  209.1 0.7 fusion.144
  209.8 2.4 custom-call.54
  214.5 0.9 fusion.212
  215.4 1.9 collective-permute-start.5
  217.3 2.4 collective-permute-start.4
  220.1 4.3 %collective-permute-done.4 = bf16[1,128,160]{1,2,0:T(8,128)(2,1)S(1)} collective-permute-done((bf16[1,128,160]{1,2,0:T(8,128)(2,1)S(1)}, bf16[1,128,160]{1,2,0:T(8,128)(2,1)S(1)}, u32[]{:S(2)}, u32[]{:S(2)}) %collective-permute-start.4) | collective-permute-done | bytes 40992 | tf_op jit(solution)/shard_map/ppermute | solution.py:15
  224.6 1.6 scatter_fusion
  226.2 1.6 scatter_fusion.1
  227.8 1.0 copy.230
  228.9 1.6 gather_fusion.7
  230.5 1.0 gather_fusion.6
  231.4 1.9 collective-permute-start.7
  233.4 2.4 collective-permute-start.6
  236.0 0.7 gather_fusion.5
  236.8 1.5 convolution_bitcast_fusion
  238.6 3.1 %collective-permute-done.6 = bf16[1,128,160]{2,1,0:T(8,128)(2,1)S(1)} collective-permute-done((bf16[1,128,160]{2,1,0:T(8,128)(2,1)S(1)}, bf16[1,128,160]{2,1,0:T(8,128)(2,1)S(1)}, u32[]{:S(2)}, u32[]{:S(2)}) %collective-permute-start.6) | collective-permute-done | bytes 40992 | tf_op jit(solution)/shard_map/ppermute | solution.py:15
  241.7 1.1 multiply_reduce_fusion
  242.8 44.1 %all-reduce.16 = (f32[160]{0:T(256)S(1)}, f32[160]{0:T(256)S(1)}) all-reduce(f32[160]{0:T(256)S(1)} %get-tuple-element.30, f32[160]{0:T(256)S(1)} %get-tuple-element.29), channel_id=1, replica_groups=mesh['grp'=4,'sub'=8] {'grp','sub'}, use_global_device_ids=true, to_apply=%region_11.15 | all-reduce | flops 320 | bytes 2560 | tf_op jit(solution)/shard_map/psum | solution.py:191
  286.9 2.3 multiply_subtract_fusion
  (250 shorter events, 19.9 us)
Async XLA Ops:
  0.6 213.9 %copy-start = (bf16[1,1024,1024]{2,1,0:T(8,128)(2,1)S(1)}, bf16[1,1024,1024]{2,1,0:T(8,128)(2,1)}, u32[]{:S(2)}) copy-start(bf16[1,1024,1024]{2,1,0:T(8,128)(2,1)} %param.27) | copy-start | bytes 6291460
  0.6 9.5 %copy-start.43 = (s32[1,6,3]{1,0,2:T(1,128)S(1)}, s32[1,6,3]{1,0,2:T(1,128)}, u32[]{:S(2)}) copy-start(s32[1,6,3]{1,0,2:T(1,128)} %param.23) | copy-start | bytes 220
  0.7 9.7 %copy-start.34 = (f32[1,32,32]{2,1,0:T(8,128)S(1)}, f32[1,32,32]{2,1,0:T(8,128)}, u32[]{:S(2)}) copy-start(f32[1,32,32]{2,1,0:T(8,128)} %param.30) | copy-start | bytes 12292
  0.7 24.5 %copy-start.35 = (f32[1,32,32]{2,1,0:T(8,128)S(1)}, f32[1,32,32]{2,1,0:T(8,128)}, u32[]{:S(2)}) copy-start(f32[1,32,32]{2,1,0:T(8,128)} %param.29) | copy-start | bytes 12292
  2.8 7.3 %copy-start.38 = (s32[128]{0:T(128)}, s32[128]{0:T(128)S(1)}, u32[]{:S(2)}) copy-start(s32[128]{0:T(128)S(1)} %get-tuple-element.52) | copy-start | bytes 1540
  2.8 22.4 %copy-start.40 = (s32[128]{0:T(128)}, s32[128]{0:T(128)S(1)}, u32[]{:S(2)}) copy-start(s32[128]{0:T(128)S(1)} %get-tuple-element.51) | copy-start | bytes 1540
  2.8 22.4 %copy-start.36 = (s32[1024]{0:T(1024)}, s32[1024]{0:T(1024)S(1)}, u32[]{:S(2)}) copy-start(s32[1024]{0:T(1024)S(1)} %get-tuple-element.59) | copy-start | bytes 12292
  2.8 22.4 %copy-start.37 = (s32[1024]{0:T(1024)}, s32[1024]{0:T(1024)S(1)}, u32[]{:S(2)}) copy-start(s32[1024]{0:T(1024)S(1)} %get-tuple-element.58) | copy-start | bytes 12292
  4.3 52.1 %collective-permute-start.1 = (bf16[1,128,160]{2,1,0:T(8,128)(2,1)}, bf16[1,128,160]{2,1,0:T(8,128)(2,1)}, u32[]{:S(2)}, u32[]{:S(2)}) collective-permute-start(bf16[1,128,160]{2,1,0:T(8,128)(2,1)} %bitcast.13), channel_id=1, source_target_pairs={{1,0},{2,1},{3,2},{4,3},{5,4},{6,5},{7,6},{8,7},{9,8},{10,9},{11,1... | collective-permute-start | bytes 122888 | tf_op jit(solution)/shard_map/ppermute | solution.py:17
  7.7 49.8 %collective-permute-start = (bf16[1,128,160]{2,1,0:T(8,128)(2,1)}, bf16[1,128,160]{2,1,0:T(8,128)(2,1)}, u32[]{:S(2)}, u32[]{:S(2)}) collective-permute-start(bf16[1,128,160]{2,1,0:T(8,128)(2,1)} %bitcast.9), channel_id=1, source_target_pairs={{0,1},{1,2},{2,3},{3,4},{4,5},{5,6},{6,7},{7,8},{8,9},{9,10},{10,1... | collective-permute-start | bytes 122888 | tf_op jit(solution)/shard_map/ppermute | solution.py:15
  10.1 43.6 %copy-start.24 = (pred[32,32]{1,0:T(8,128)(4,1)}, pred[32,32]{1,0:T(8,128)(4,1)S(1)}, u32[]{:S(2)}) copy-start(pred[32,32]{1,0:T(8,128)(4,1)S(1)} %iota_compare_fusion.3) | copy-start | bytes 3076
  10.2 45.5 %copy-start.22 = (pred[32,32]{1,0:T(8,128)(4,1)}, pred[32,32]{1,0:T(8,128)(4,1)S(1)}, u32[]{:S(2)}) copy-start(pred[32,32]{1,0:T(8,128)(4,1)S(1)} %iota_compare_fusion.7) | copy-start | bytes 3076
  10.4 43.3 %copy-start.30 = (s32[1024]{0:T(1024)}, s32[1024]{0:T(1024)S(1)}, u32[]{:S(2)}) copy-start(s32[1024]{0:T(1024)S(1)} %pad_clamp_fusion.2) | copy-start | bytes 12292
  39.2 12.7 %copy-start.11 = (f32[8,32,32]{2,1,0:T(8,128)}, f32[8,32,32]{2,1,0:T(8,128)S(1)}, u32[]{:S(2)}) copy-start(f32[8,32,32]{2,1,0:T(8,128)S(1)} %all_gather.30) | copy-start | bytes 98308
  51.2 0.7 copy-start.15
  51.9 1.8 copy-start.5
  53.7 2.0 copy-start.16
  53.7 2.0 copy-start.42
  53.7 2.7 copy-start.9
  53.7 3.8 %copy-start.1 = (f32[768,160]{0,1:T(8,128)S(1)}, f32[768,160]{0,1:T(8,128)}, u32[]{:S(2)}) copy-start(f32[768,160]{0,1:T(8,128)} %param.20) | copy-start | bytes 1474564
  53.7 3.8 %copy-start.7 = (bf16[768,128]{1,0:T(8,128)(2,1)S(1)}, bf16[768,128]{1,0:T(8,128)(2,1)}, u32[]{:S(2)}) copy-start(bf16[768,128]{1,0:T(8,128)(2,1)} %param.24) | copy-start | bytes 589828
  53.7 3.8 %copy-start.12 = (f32[768,160]{0,1:T(8,128)S(1)}, f32[768,160]{0,1:T(8,128)}, u32[]{:S(2)}) copy-start(f32[768,160]{0,1:T(8,128)} %param.19) | copy-start | bytes 1474564
  53.7 3.8 %copy-start.32 = (f32[768]{0:T(1024)S(1)}, f32[768]{0:T(1024)}, u32[]{:S(2)}) copy-start(f32[768]{0:T(1024)} %param.21) | copy-start | bytes 9220
  56.4 46.9 %copy-start.13 = (f32[1,32,32]{2,1,0:T(8,128)}, f32[1,32,32]{2,1,0:T(8,128)S(1)}, u32[]{:S(2)}) copy-start(f32[1,32,32]{2,1,0:T(8,128)S(1)} %get-tuple-element.38) | copy-start | bytes 12292
  59.5 20.4 %slice-start.1 = ((f32[8,32,32]{2,1,0:T(8,128)}), f32[1,32,32]{2,1,0:T(8,128)S(1)}, s32[]{:S(2)}) async-start(f32[8,32,32]{2,1,0:T(8,128)} %copy-done.11), calls=%async_computation.1 | async-start | bytes 32768 | tf_op jit(solution)/shard_map/slice | solution.py:161
  59.6 30.7 %copy-start.20 = (bf16[1,1024,32]{1,2,0:T(8,128)(2,1)S(1)}, bf16[1,1024,32]{1,2,0:T(8,128)(2,1)}, u32[]{:S(2)}) copy-start(bf16[1,1024,32]{1,2,0:T(8,128)(2,1)} %param.28) | copy-start | bytes 196612
  61.8 27.9 %collective-permute-start.3 = (bf16[1,128,160]{1,2,0:T(8,128)(2,1)S(1)}, bf16[1,128,160]{1,2,0:T(8,128)(2,1)S(1)}, u32[]{:S(2)}, u32[]{:S(2)}) collective-permute-start(bf16[1,128,160]{1,2,0:T(8,128)(2,1)S(1)} %bitcast.412), channel_id=1, source_target_pairs={{1,0},{2,1},{3,2},{4,3},{5,4},{6,5},{7,6},{8,7},{9,8},{10,9},{11,1... | collective-permute-start | bytes 122888 | tf_op jit(solution)/shard_map/ppermute | solution.py:17
  65.9 23.7 %collective-permute-start.2 = (bf16[1,128,160]{1,2,0:T(8,128)(2,1)S(1)}, bf16[1,128,160]{1,2,0:T(8,128)(2,1)S(1)}, u32[]{:S(2)}, u32[]{:S(2)}) collective-permute-start(bf16[1,128,160]{1,2,0:T(8,128)(2,1)S(1)} %bitcast.413), channel_id=1, source_target_pairs={{0,1},{1,2},{2,3},{3,4},{4,5},{5,6},{6,7},{7,8},{8,9},{9,10},{10,1... | collective-permute-start | bytes 122888 | tf_op jit(solution)/shard_map/ppermute | solution.py:15
  89.7 0.6 copy-start.26
  89.7 0.6 copy-start.28
  90.3 13.0 %copy-start.18 = (f32[4,1,32,32]{2,3,1,0:T(8,128)S(1)}, f32[4,1,32,32]{2,3,1,0:T(8,128)}, u32[]{:S(2)}) copy-start(f32[4,1,32,32]{2,3,1,0:T(8,128)} %custom-call.48) | copy-start | bytes 49156
  90.3 13.1 %copy-start.19 = (f32[4,32,32]{2,1,0:T(8,128)S(1)}, f32[4,32,32]{2,1,0:T(8,128)}, u32[]{:S(2)}) copy-start(f32[4,32,32]{2,1,0:T(8,128)} %copy.187) | copy-start | bytes 49156
  103.2 1.0 copy-start.6
  104.5 7.3 %copy-start.25 = (pred[32,32]{1,0:T(8,128)(4,1)S(1)}, pred[32,32]{1,0:T(8,128)(4,1)}, u32[]{:S(2)}) copy-start(pred[32,32]{1,0:T(8,128)(4,1)} %copy-done.24) | copy-start | bytes 3076
  104.5 7.5 %copy-start.23 = (pred[32,32]{1,0:T(8,128)(4,1)S(1)}, pred[32,32]{1,0:T(8,128)(4,1)}, u32[]{:S(2)}) copy-start(pred[32,32]{1,0:T(8,128)(4,1)} %copy-done.22) | copy-start | bytes 3076
  134.6 0.9 copy-start.14
  134.6 1.9 slice-start
  135.2 33.1 %copy-start.44 = (pred[4]{0:T(512)(128)(4,1)S(1)}, pred[4]{0:T(512)(128)(4,1)}, u32[]{:S(2)}) copy-start(pred[4]{0:T(512)(128)(4,1)} %constant.263.clone.1) | copy-start | bytes 16
  152.4 32.1 %copy-start.17 = (f32[4,32,32]{1,2,0:T(8,128)S(1)}, f32[4,32,32]{1,2,0:T(8,128)}, u32[]{:S(2)}) copy-start(f32[4,32,32]{1,2,0:T(8,128)} %copy.210) | copy-start | bytes 49156
  212.5 1.7 copy-start.21
  213.3 1.2 copy-start.27
  213.3 1.2 copy-start.29
  215.4 4.7 %collective-permute-start.5 = (bf16[1,128,160]{1,2,0:T(8,128)(2,1)S(1)}, bf16[1,128,160]{1,2,0:T(8,128)(2,1)S(1)}, u32[]{:S(2)}, u32[]{:S(2)}) collective-permute-start(bf16[1,128,160]{1,2,0:T(8,128)(2,1)S(1)} %get-tuple-element.34), channel_id=1, source_target_pairs={{1,0},{2,1},{3,2},{4,3},{5,4},{6,5},{7,6},{8,7},{9,8},{10,9},{11,1... | collective-permute-start | bytes 122888 | tf_op jit(solution)/shard_map/ppermute | solution.py:17
  217.3 7.1 %collective-permute-start.4 = (bf16[1,128,160]{1,2,0:T(8,128)(2,1)S(1)}, bf16[1,128,160]{1,2,0:T(8,128)(2,1)S(1)}, u32[]{:S(2)}, u32[]{:S(2)}) collective-permute-start(bf16[1,128,160]{1,2,0:T(8,128)(2,1)S(1)} %get-tuple-element.33), channel_id=1, source_target_pairs={{0,1},{1,2},{2,3},{3,4},{4,5},{5,6},{6,7},{7,8},{8,9},{9,10},{10,1... | collective-permute-start | bytes 122888 | tf_op jit(solution)/shard_map/ppermute | solution.py:15
  219.8 4.8 %copy-start.41 = (s32[128]{0:T(128)S(1)}, s32[128]{0:T(128)}, u32[]{:S(2)}) copy-start(s32[128]{0:T(128)} %copy-done.40) | copy-start | bytes 1540
  224.5 1.7 copy-start.39
  228.9 7.1 %copy-start.31 = (s32[1024]{0:T(1024)S(1)}, s32[1024]{0:T(1024)}, u32[]{:S(2)}) copy-start(s32[1024]{0:T(1024)} %copy-done.30) | copy-start | bytes 12292
  231.4 6.9 %collective-permute-start.7 = (bf16[1,128,160]{2,1,0:T(8,128)(2,1)}, bf16[1,128,160]{2,1,0:T(8,128)(2,1)S(1)}, u32[]{:S(2)}, u32[]{:S(2)}) collective-permute-start(bf16[1,128,160]{2,1,0:T(8,128)(2,1)} %bitcast.124), channel_id=1, source_target_pairs={{1,0},{2,1},{3,2},{4,3},{5,4},{6,5},{7,6},{8,7},{9,8},{10,9},{11,1... | collective-permute-start | bytes 122888 | tf_op jit(solution)/shard_map/ppermute | solution.py:17
  233.4 8.3 %collective-permute-start.6 = (bf16[1,128,160]{2,1,0:T(8,128)(2,1)S(1)}, bf16[1,128,160]{2,1,0:T(8,128)(2,1)S(1)}, u32[]{:S(2)}, u32[]{:S(2)}) collective-permute-start(bf16[1,128,160]{2,1,0:T(8,128)(2,1)S(1)} %bitcast.407), channel_id=1, source_target_pairs={{0,1},{1,2},{2,3},{3,4},{4,5},{5,6},{6,7},{7,8},{8,9},{9,10},{10,1... | collective-permute-start | bytes 122888 | tf_op jit(solution)/shard_map/ppermute | solution.py:15
  236.7 1.6 copy-start.10
  236.7 4.9 %copy-start.3 = (f32[768,160]{0,1:T(8,128)S(1)}, f32[768,160]{0,1:T(8,128)}, u32[]{:S(2)}) copy-start(f32[768,160]{0,1:T(8,128)} %get-tuple-element.54) | copy-start | bytes 1474564
  236.7 4.9 %copy-start.4 = (f32[768,160]{0,1:T(8,128)S(1)}, f32[768,160]{0,1:T(8,128)}, u32[]{:S(2)}) copy-start(f32[768,160]{0,1:T(8,128)} %copy.230) | copy-start | bytes 1474564
  236.7 4.9 %copy-start.8 = (bf16[768,128]{1,0:T(8,128)(2,1)S(1)}, bf16[768,128]{1,0:T(8,128)(2,1)}, u32[]{:S(2)}) copy-start(bf16[768,128]{1,0:T(8,128)(2,1)} %param.24) | copy-start | bytes 589828
  236.8 4.9 %copy-start.33 = (f32[768]{0:T(1024)S(1)}, f32[768]{0:T(1024)}, u32[]{:S(2)}) copy-start(f32[768]{0:T(1024)} %param.21) | copy-start | bytes 9220
  241.7 45.2 %copy-start.2 = (f32[768,160]{0,1:T(8,128)S(1)}, f32[768,160]{0,1:T(8,128)}, u32[]{:S(2)}) copy-start(f32[768,160]{0,1:T(8,128)} %param.20) | copy-start | bytes 1474564
where the time goes:
time: 290 us; the launch traced here: 289 us
  blocking collectives  142 us (49%)
  other arithmetic  79.4 us (27%)
  matrix products  21.8 us (8%)
  starting transfers between devices  18.9 us (7%)
  local copies, waits for them, and re-layouts  17.4 us (6%)
  waiting for transfers between devices  7.38 us (3%)
    psum x1, blocking collectives, shards(): inner = lax.psum(jnp.sum(residual_start * owned, axis=0), ('grp', 'sub'))  44.1 us
    another operation x15, other arithmetic, chol_solve(): lax.linalg.triangular_solve(factor, halfway, left_side=True, lower=True,...  34 us
    another operation x15, other arithmetic, solve_chain(): factor = jnp.linalg.cholesky(diag_odd)  31.6 us
    all_gather x1, blocking collectives, shards(): blocks_up = lax.all_gather(coarse_up, 'sub', axis=0, tiled=True)  14.8 us
    all_gather x1, blocking collectives, shards(): blocks_diag = lax.all_gather(coarse_diag, 'sub', axis=0, tiled=True)  14 us
    all_gather x1, blocking collectives, shards(): columns = lax.all_gather(coarse_in[None], 'sub', axis=0, tiled=True)  12.7 us
    ppermute x4, starting transfers between devices, with_halo(): lax.ppermute(head, axis, [((i + 1) % count, i) for i in range(ends)])  9.75 us
    ppermute x4, starting transfers between devices, with_halo(): lax.ppermute(tail, axis, [(i, (i + 1) % count) for i in range(ends)])  9.13 us
  transfers between devices with their start and end apart: 8, of which 2 were waited for; matrix products, arithmetic and copies ran while one was open for 12% of the time, Pallas kernels for 0%

commit v1 on v0

--- a/solution.py
+++ b/solution.py
@@ -2,6 +2,8 @@
 import jax.numpy as jnp
 from jax import lax
 from jax.sharding import PartitionSpec as P
+
+serve_rounds = lambda tile_in: lax.psum(lax.psum(tile_in, "sub"), axis_name="grp")
 
 
 def with_halo(cells, sides, width):
@@ -188,7 +190,7 @@
     owned = correction[intersection : intersection + rows_own]
     owned = owned.at[sent_right_rows].add(returned[3])
     owned = owned.at[sent_left_rows].add(returned[0])
-    inner = lax.psum(jnp.sum(residual_start * owned, axis=0), ("grp", "sub"))
+    inner = serve_rounds(jnp.sum(residual_start * owned, axis=0))
     image = apply_operator(owned)
     curvature = lax.psum(jnp.sum(owned * image, axis=0), ("grp", "sub"))
     step_size = inner / curvature

time: 290 us -> 313 us (1.079)
  blocking collectives: 142 us -> 165 us
    psum x1 -> x3, blocking collectives: 44.1 us -> 66.6 us  [the longest x1 43.5 us: shards(): curvature = lax.psum(jnp.sum(owned * image, axis=0), ('grp', 'sub'))]
  transfers between devices with their start and end apart: 8 -> 8, of which waited for: 2 -> 2; matrix products, arithmetic and copies ran while one was open for 12% -> 11% of each run, Pallas kernels for 0% -> 0%
where the time goes in v1:
time: 313 us; the launch traced here: 312 us
  blocking collectives  165 us (53%)
  other arithmetic  79.4 us (25%)
  matrix products  21.8 us (7%)
  starting transfers between devices  18.9 us (6%)
  local copies, waits for them, and re-layouts  17.5 us (6%)
  waiting for transfers between devices  7.4 us (2%)
    psum x1, blocking collectives, shards(): curvature = lax.psum(jnp.sum(owned * image, axis=0), ('grp', 'sub'))  43.5 us
    another operation x15, other arithmetic, chol_solve(): lax.linalg.triangular_solve(factor, halfway, left_side=True, lower=True,...  34 us
    another operation x15, other arithmetic, solve_chain(): factor = jnp.linalg.cholesky(diag_odd)  31.6 us
    all_gather x1, blocking collectives, shards(): blocks_up = lax.all_gather(coarse_up, 'sub', axis=0, tiled=True)  14.8 us
    all_gather x1, blocking collectives, shards(): blocks_diag = lax.all_gather(coarse_diag, 'sub', axis=0, tiled=True)  14 us
    psum x1, blocking collectives, lax.psum(tile_in, 'sub')  13.9 us
    all_gather x1, blocking collectives, shards(): columns = lax.all_gather(coarse_in[None], 'sub', axis=0, tiled=True)  12.7 us
    ppermute x4, starting transfers between devices, with_halo(): lax.ppermute(head, axis, [((i + 1) % count, i) for i in range(ends)])  9.75 us
  transfers between devices with their start and end apart: 8, of which 2 were waited for; matrix products, arithmetic and copies ran while one was open for 11% of the time, Pallas kernels for 0%

profile of v1, /device:TPU:14, one launch (start us, length us, event | category | flops | bytes accessed | tf_op | source)
XLA Modules:
  0.0 311.8 jit_solution(4640427087524515887)
XLA Ops:
  0.7 1.3 copy.175
  2.0 0.8 fusion.182
  2.8 1.5 gather_fusion.2
  4.3 1.9 collective-permute-start.1
  6.2 1.5 gather_fusion.1
  7.7 2.4 collective-permute-start
  10.4 14.8 %all_gather.32 = f32[8,32,32]{2,1,0:T(8,128)S(1)} all-gather(f32[1,32,32]{2,1,0:T(8,128)S(1)} %copy-done.34), channel_id=1, replica_groups=mesh['grp'=4,'sub'=8] {'sub'}, dimensions={0}, use_global_device_ids=true | all-gather | bytes 36864 | tf_op jit(solution)/shard_map/all_gather | solution.py:139
  25.2 14.0 %all_gather.30 = f32[8,32,32]{2,1,0:T(8,128)S(1)} all-gather(f32[1,32,32]{2,1,0:T(8,128)S(1)} %copy-done.35), channel_id=1, replica_groups=mesh['grp'=4,'sub'=8] {'sub'}, dimensions={0}, use_global_device_ids=true | all-gather | bytes 36864 | tf_op jit(solution)/shard_map/all_gather | solution.py:138
  39.5 11.7 %custom-call.47 = f32[4,32,32]{2,1,0:T(8,128)S(1)} custom-call(f32[4,32,32]{2,1,0:T(8,128)S(1)} %copy.185), custom_call_target="Cholesky" | custom-call | tf_op jit(solution)/shard_map/jit(cholesky)/cholesky | solution.py:57
  51.3 0.7 compare_reduce_fusion.6
  52.0 1.7 gather_fusion
  53.8 1.9 convolution_bitcast_fusion.1
  55.7 0.7 select_bitcast_fusion
  56.4 1.1 fusion.73
  57.6 1.9 fusion.211
  59.7 1.1 gather_fusion.4
  60.8 1.0 gather_fusion.3
  61.9 4.0 %collective-permute-start.3 = (bf16[1,128,160]{1,2,0:T(8,128)(2,1)S(1)}, bf16[1,128,160]{1,2,0:T(8,128)(2,1)S(1)}, u32[]{:S(2)}, u32[]{:S(2)}) collective-permute-start(bf16[1,128,160]{1,2,0:T(8,128)(2,1)S(1)} %bitcast.412), channel_id=1, source_target_pairs={{1,0},{2,1},{3,2},{4,3},{5,4},{6,5},{7,6},{8,7},{9,8},{10,9},{11,1... | collective-permute-start | bytes 122888 | tf_op jit(solution)/shard_map/ppermute | solution.py:19
  66.0 1.9 collective-permute-start.2
  68.0 0.7 copy.187
  68.7 11.2 %custom-call.48 = f32[4,1,32,32]{2,3,1,0:T(8,128)} custom-call(f32[4,1,32,32]{3,2,1,0:T(8,128)} %select_bitcast_fusion), custom_call_target="InvertDiagBlocksLowerTriangular" | custom-call | tf_op jit(solution)/shard_map/triangular_solve | solution.py:28
  79.9 9.1 %all_gather.31 = f32[4,32,32]{2,1,0:T(8,128)S(1)} all-gather(f32[1,32,32]{2,1,0:T(8,128)S(1)} %slice-done.1), channel_id=1, replica_groups=mesh['grp'=4,'sub'=8] {'grp'}, dimensions={0}, use_global_device_ids=true | all-gather | bytes 20480 | tf_op jit(solution)/shard_map/all_gather | solution.py:163
  89.0 0.7 copy.210
  90.6 12.7 %all-gather = f32[256,160]{1,0:T(8,128)S(1)} all-gather(f32[32,160]{1,0:T(8,128)S(1)} %convolution_bitcast_fusion.11), channel_id=2, replica_groups=mesh['grp'=4,'sub'=8] {'sub'}, dimensions={0}, use_global_device_ids=true | all-gather | bytes 184320 | tf_op jit(solution)/shard_map/all_gather | solution.py:147
  106.1 5.9 %custom-call.57 = f32[2,32,32]{2,1,0:T(8,128)S(1)} custom-call(f32[2,32,32]{2,1,0:T(8,128)S(1)} %fusion.117), custom_call_target="Cholesky" | custom-call | tf_op jit(solution)/shard_map/jit(cholesky)/cholesky | solution.py:57
  112.2 4.9 %custom-call.49 = f32[2,1,32,32]{2,3,1,0:T(8,128)S(1)} custom-call(f32[2,1,32,32]{3,2,1,0:T(8,128)S(1)} %fusion.119), custom_call_target="InvertDiagBlocksLowerTriangular" | custom-call | tf_op jit(solution)/shard_map/triangular_solve | solution.py:28
  119.2 2.9 custom-call.58
  123.3 2.4 custom-call.50
  127.0 2.9 cholesky.184
  131.1 2.4 custom-call.51
  136.5 7.0 %all-gather.6 = f32[128,160]{1,0:T(8,128)S(1)} all-gather(f32[32,160]{1,0:T(8,128)S(1)} %slice-done), channel_id=8, replica_groups=mesh['grp'=4,'sub'=8] {'grp'}, dimensions={0}, use_global_device_ids=true | all-gather | bytes 102400 | tf_op jit(solution)/shard_map/all_gather | solution.py:164
  143.5 8.9 %all-gather.4 = f32[128,160]{1,0:T(8,128)S(1)} all-gather(f32[32,160]{1,0:T(8,128)S(1)} %convolution_bitcast_fusion.7), channel_id=6, replica_groups=mesh['grp'=4,'sub'=8] {'grp'}, dimensions={0}, use_global_device_ids=true | all-gather | bytes 102400 | tf_op jit(solution)/shard_map/all_gather | solution.py:168
  152.5 7.1 %all-gather.5 = f32[128,160]{1,0:T(8,128)S(1)} all-gather(f32[32,160]{1,0:T(8,128)S(1)} %fusion.101), channel_id=7, replica_groups=mesh['grp'=4,'sub'=8] {'grp'}, dimensions={0}, use_global_device_ids=true | all-gather | bytes 102400 | tf_op jit(solution)/shard_map/all_gather | solution.py:169
  159.7 8.7 %all-gather.3 = f32[128,32]{1,0:T(8,128)S(1)} all-gather(f32[32,32]{1,0:T(8,128)S(1)} %copy.214), channel_id=5, replica_groups=mesh['grp'=4,'sub'=8] {'grp'}, dimensions={0}, use_global_device_ids=true | all-gather | bytes 20480 | tf_op jit(solution)/shard_map/all_gather | solution.py:167
  168.6 6.7 %all-gather.2 = f32[128,32]{1,0:T(8,128)S(1)} all-gather(f32[32,32]{1,0:T(8,128)S(1)} %fusion.145), channel_id=4, replica_groups=mesh['grp'=4,'sub'=8] {'grp'}, dimensions={0}, use_global_device_ids=true | all-gather | bytes 20480 | tf_op jit(solution)/shard_map/all_gather | solution.py:166
  175.5 8.9 %all-gather.1 = f32[128,32]{1,0:T(8,128)S(1)} all-gather(f32[32,32]{1,0:T(8,128)S(1)} %copy.208), channel_id=3, replica_groups=mesh['grp'=4,'sub'=8] {'grp'}, dimensions={0}, use_global_device_ids=true | all-gather | bytes 20480 | tf_op jit(solution)/shard_map/all_gather | solution.py:165
  184.7 5.9 %custom-call.59 = f32[2,32,32]{2,1,0:T(8,128)S(1)} custom-call(f32[2,32,32]{2,1,0:T(8,128)S(1)} %fusion.112), custom_call_target="Cholesky" | custom-call | tf_op jit(solution)/shard_map/jit(cholesky)/cholesky | solution.py:57
  190.8 4.9 %custom-call.52 = f32[2,1,32,32]{2,3,1,0:T(8,128)S(1)} custom-call(f32[2,1,32,32]{3,2,1,0:T(8,128)S(1)} %fusion.118), custom_call_target="InvertDiagBlocksLowerTriangular" | custom-call | tf_op jit(solution)/shard_map/triangular_solve | solution.py:28
  197.7 2.9 custom-call.60
  200.7 0.6 compare_reduce_fusion.1
  201.3 0.7 fusion.143
  202.0 2.4 custom-call.53
  205.6 2.9 cholesky.216
  209.2 0.7 fusion.144
  209.9 2.4 custom-call.54
  214.6 0.9 fusion.212
  215.5 1.9 collective-permute-start.5
  217.4 2.4 collective-permute-start.4
  220.1 4.3 %collective-permute-done.4 = bf16[1,128,160]{1,2,0:T(8,128)(2,1)S(1)} collective-permute-done((bf16[1,128,160]{1,2,0:T(8,128)(2,1)S(1)}, bf16[1,128,160]{1,2,0:T(8,128)(2,1)S(1)}, u32[]{:S(2)}, u32[]{:S(2)}) %collective-permute-start.4) | collective-permute-done | bytes 40992 | tf_op jit(solution)/shard_map/ppermute | solution.py:17
  224.7 1.6 scatter_fusion
  226.3 1.6 scatter_fusion.1
  227.9 1.0 copy.230
  229.0 1.6 gather_fusion.7
  230.6 1.0 gather_fusion.6
  231.5 1.9 collective-permute-start.7
  233.5 2.4 collective-permute-start.6
  236.1 0.7 gather_fusion.5
  236.9 1.5 convolution_bitcast_fusion
  238.7 3.1 collective-permute-done.6
  241.8 1.1 multiply_reduce_fusion
  242.9 13.9 %psum.21 = f32[160]{0:T(256)S(1)} all-reduce(f32[160]{0:T(256)S(1)} %get-tuple-element.30), channel_id=1, replica_groups=mesh['grp'=4,'sub'=8] {'sub'}, use_global_device_ids=true, to_apply=%region_11.15 | all-reduce | flops 160 | bytes 1280 | tf_op jit(solution)/shard_map/psum | solution.py:6
  256.8 9.3 %psum.22 = f32[160]{0:T(256)S(1)} all-reduce(f32[160]{0:T(256)S(1)} %psum.21), channel_id=1, replica_groups=mesh['grp'=4,'sub'=8] {'grp'}, use_global_device_ids=true, to_apply=%region_12.16 | all-reduce | flops 160 | bytes 1280 | tf_op jit(solution)/shard_map/psum | solution.py:6
  266.0 43.5 %psum.23 = f32[160]{0:T(256)S(1)} all-reduce(f32[160]{0:T(256)S(1)} %get-tuple-element.29), channel_id=1, replica_groups=mesh['grp'=4,'sub'=8] {'grp','sub'}, use_global_device_ids=true, to_apply=%region_14.18 | all-reduce | flops 160 | bytes 1280 | tf_op jit(solution)/shard_map/psum | solution.py:195
  309.5 2.3 multiply_subtract_fusion
  (252 shorter events, 21.2 us)
Async XLA Ops:
  0.6 213.9 %copy-start = (bf16[1,1024,1024]{2,1,0:T(8,128)(2,1)S(1)}, bf16[1,1024,1024]{2,1,0:T(8,128)(2,1)}, u32[]{:S(2)}) copy-start(bf16[1,1024,1024]{2,1,0:T(8,128)(2,1)} %param.27) | copy-start | bytes 6291460
  0.6 9.5 %copy-start.43 = (s32[1,6,3]{1,0,2:T(1,128)S(1)}, s32[1,6,3]{1,0,2:T(1,128)}, u32[]{:S(2)}) copy-start(s32[1,6,3]{1,0,2:T(1,128)} %param.23) | copy-start | bytes 220
  0.7 9.7 %copy-start.34 = (f32[1,32,32]{2,1,0:T(8,128)S(1)}, f32[1,32,32]{2,1,0:T(8,128)}, u32[]{:S(2)}) copy-start(f32[1,32,32]{2,1,0:T(8,128)} %param.30) | copy-start | bytes 12292
  0.7 24.5 %copy-start.35 = (f32[1,32,32]{2,1,0:T(8,128)S(1)}, f32[1,32,32]{2,1,0:T(8,128)}, u32[]{:S(2)}) copy-start(f32[1,32,32]{2,1,0:T(8,128)} %param.29) | copy-start | bytes 12292
  2.8 7.3 %copy-start.38 = (s32[128]{0:T(128)}, s32[128]{0:T(128)S(1)}, u32[]{:S(2)}) copy-start(s32[128]{0:T(128)S(1)} %get-tuple-element.50) | copy-start | bytes 1540
  2.8 22.4 %copy-start.40 = (s32[128]{0:T(128)}, s32[128]{0:T(128)S(1)}, u32[]{:S(2)}) copy-start(s32[128]{0:T(128)S(1)} %get-tuple-element.49) | copy-start | bytes 1540
  2.8 22.4 %copy-start.36 = (s32[1024]{0:T(1024)}, s32[1024]{0:T(1024)S(1)}, u32[]{:S(2)}) copy-start(s32[1024]{0:T(1024)S(1)} %get-tuple-element.57) | copy-start | bytes 12292
  2.8 22.4 %copy-start.37 = (s32[1024]{0:T(1024)}, s32[1024]{0:T(1024)S(1)}, u32[]{:S(2)}) copy-start(s32[1024]{0:T(1024)S(1)} %get-tuple-element.56) | copy-start | bytes 12292
  4.3 52.1 %collective-permute-start.1 = (bf16[1,128,160]{2,1,0:T(8,128)(2,1)}, bf16[1,128,160]{2,1,0:T(8,128)(2,1)}, u32[]{:S(2)}, u32[]{:S(2)}) collective-permute-start(bf16[1,128,160]{2,1,0:T(8,128)(2,1)} %bitcast.13), channel_id=1, source_target_pairs={{1,0},{2,1},{3,2},{4,3},{5,4},{6,5},{7,6},{8,7},{9,8},{10,9},{11,1... | collective-permute-start | bytes 122888 | tf_op jit(solution)/shard_map/ppermute | solution.py:19
  7.7 49.9 %collective-permute-start = (bf16[1,128,160]{2,1,0:T(8,128)(2,1)}, bf16[1,128,160]{2,1,0:T(8,128)(2,1)}, u32[]{:S(2)}, u32[]{:S(2)}) collective-permute-start(bf16[1,128,160]{2,1,0:T(8,128)(2,1)} %bitcast.9), channel_id=1, source_target_pairs={{0,1},{1,2},{2,3},{3,4},{4,5},{5,6},{6,7},{7,8},{8,9},{9,10},{10,1... | collective-permute-start | bytes 122888 | tf_op jit(solution)/shard_map/ppermute | solution.py:17
  10.1 43.6 %copy-start.24 = (pred[32,32]{1,0:T(8,128)(4,1)}, pred[32,32]{1,0:T(8,128)(4,1)S(1)}, u32[]{:S(2)}) copy-start(pred[32,32]{1,0:T(8,128)(4,1)S(1)} %iota_compare_fusion.3) | copy-start | bytes 3076
  10.2 45.5 %copy-start.22 = (pred[32,32]{1,0:T(8,128)(4,1)}, pred[32,32]{1,0:T(8,128)(4,1)S(1)}, u32[]{:S(2)}) copy-start(pred[32,32]{1,0:T(8,128)(4,1)S(1)} %iota_compare_fusion.7) | copy-start | bytes 3076
  10.4 43.3 %copy-start.30 = (s32[1024]{0:T(1024)}, s32[1024]{0:T(1024)S(1)}, u32[]{:S(2)}) copy-start(s32[1024]{0:T(1024)S(1)} %pad_clamp_fusion.2) | copy-start | bytes 12292
  39.2 12.8 %copy-start.11 = (f32[8,32,32]{2,1,0:T(8,128)}, f32[8,32,32]{2,1,0:T(8,128)S(1)}, u32[]{:S(2)}) copy-start(f32[8,32,32]{2,1,0:T(8,128)S(1)} %all_gather.30) | copy-start | bytes 98308
  51.2 0.7 copy-start.15
  52.0 1.8 copy-start.5
  53.7 2.0 copy-start.16
  53.7 2.0 copy-start.42
  53.7 2.7 copy-start.9
  53.7 3.8 %copy-start.1 = (f32[768,160]{0,1:T(8,128)S(1)}, f32[768,160]{0,1:T(8,128)}, u32[]{:S(2)}) copy-start(f32[768,160]{0,1:T(8,128)} %param.20) | copy-start | bytes 1474564
  53.7 3.8 %copy-start.7 = (bf16[768,128]{1,0:T(8,128)(2,1)S(1)}, bf16[768,128]{1,0:T(8,128)(2,1)}, u32[]{:S(2)}) copy-start(bf16[768,128]{1,0:T(8,128)(2,1)} %param.24) | copy-start | bytes 589828
  53.8 3.8 %copy-start.12 = (f32[768,160]{0,1:T(8,128)S(1)}, f32[768,160]{0,1:T(8,128)}, u32[]{:S(2)}) copy-start(f32[768,160]{0,1:T(8,128)} %param.19) | copy-start | bytes 1474564
  53.8 3.8 %copy-start.32 = (f32[768]{0:T(1024)S(1)}, f32[768]{0:T(1024)}, u32[]{:S(2)}) copy-start(f32[768]{0:T(1024)} %param.21) | copy-start | bytes 9220
  56.4 46.9 %copy-start.13 = (f32[1,32,32]{2,1,0:T(8,128)}, f32[1,32,32]{2,1,0:T(8,128)S(1)}, u32[]{:S(2)}) copy-start(f32[1,32,32]{2,1,0:T(8,128)S(1)} %get-tuple-element.36) | copy-start | bytes 12292
  59.5 20.4 %slice-start.1 = ((f32[8,32,32]{2,1,0:T(8,128)}), f32[1,32,32]{2,1,0:T(8,128)S(1)}, s32[]{:S(2)}) async-start(f32[8,32,32]{2,1,0:T(8,128)} %copy-done.11), calls=%async_computation.1 | async-start | bytes 32768 | tf_op jit(solution)/shard_map/slice | solution.py:163
  59.7 30.7 %copy-start.20 = (bf16[1,1024,32]{1,2,0:T(8,128)(2,1)S(1)}, bf16[1,1024,32]{1,2,0:T(8,128)(2,1)}, u32[]{:S(2)}) copy-start(bf16[1,1024,32]{1,2,0:T(8,128)(2,1)} %param.28) | copy-start | bytes 196612
  61.9 27.9 %collective-permute-start.3 = (bf16[1,128,160]{1,2,0:T(8,128)(2,1)S(1)}, bf16[1,128,160]{1,2,0:T(8,128)(2,1)S(1)}, u32[]{:S(2)}, u32[]{:S(2)}) collective-permute-start(bf16[1,128,160]{1,2,0:T(8,128)(2,1)S(1)} %bitcast.412), channel_id=1, source_target_pairs={{1,0},{2,1},{3,2},{4,3},{5,4},{6,5},{7,6},{8,7},{9,8},{10,9},{11,1... | collective-permute-start | bytes 122888 | tf_op jit(solution)/shard_map/ppermute | solution.py:19
  66.0 23.8 %collective-permute-start.2 = (bf16[1,128,160]{1,2,0:T(8,128)(2,1)S(1)}, bf16[1,128,160]{1,2,0:T(8,128)(2,1)S(1)}, u32[]{:S(2)}, u32[]{:S(2)}) collective-permute-start(bf16[1,128,160]{1,2,0:T(8,128)(2,1)S(1)} %bitcast.413), channel_id=1, source_target_pairs={{0,1},{1,2},{2,3},{3,4},{4,5},{5,6},{6,7},{7,8},{8,9},{9,10},{10,1... | collective-permute-start | bytes 122888 | tf_op jit(solution)/shard_map/ppermute | solution.py:17
  89.7 0.6 copy-start.26
  89.8 0.6 copy-start.28
  90.4 13.0 %copy-start.18 = (f32[4,1,32,32]{2,3,1,0:T(8,128)S(1)}, f32[4,1,32,32]{2,3,1,0:T(8,128)}, u32[]{:S(2)}) copy-start(f32[4,1,32,32]{2,3,1,0:T(8,128)} %custom-call.48) | copy-start | bytes 49156
  90.4 13.1 %copy-start.19 = (f32[4,32,32]{2,1,0:T(8,128)S(1)}, f32[4,32,32]{2,1,0:T(8,128)}, u32[]{:S(2)}) copy-start(f32[4,32,32]{2,1,0:T(8,128)} %copy.187) | copy-start | bytes 49156
  103.3 0.9 copy-start.6
  104.6 7.3 %copy-start.25 = (pred[32,32]{1,0:T(8,128)(4,1)S(1)}, pred[32,32]{1,0:T(8,128)(4,1)}, u32[]{:S(2)}) copy-start(pred[32,32]{1,0:T(8,128)(4,1)} %copy-done.24) | copy-start | bytes 3076
  104.6 7.5 %copy-start.23 = (pred[32,32]{1,0:T(8,128)(4,1)S(1)}, pred[32,32]{1,0:T(8,128)(4,1)}, u32[]{:S(2)}) copy-start(pred[32,32]{1,0:T(8,128)(4,1)} %copy-done.22) | copy-start | bytes 3076
  134.6 0.9 copy-start.14
  134.7 1.9 slice-start
  135.3 33.1 %copy-start.44 = (pred[4]{0:T(512)(128)(4,1)S(1)}, pred[4]{0:T(512)(128)(4,1)}, u32[]{:S(2)}) copy-start(pred[4]{0:T(512)(128)(4,1)} %constant.263.clone.1) | copy-start | bytes 16
  152.5 32.1 %copy-start.17 = (f32[4,32,32]{1,2,0:T(8,128)S(1)}, f32[4,32,32]{1,2,0:T(8,128)}, u32[]{:S(2)}) copy-start(f32[4,32,32]{1,2,0:T(8,128)} %copy.210) | copy-start | bytes 49156
  212.6 1.7 copy-start.21
  213.4 1.2 copy-start.27
  213.4 1.2 copy-start.29
  215.5 4.7 %collective-permute-start.5 = (bf16[1,128,160]{1,2,0:T(8,128)(2,1)S(1)}, bf16[1,128,160]{1,2,0:T(8,128)(2,1)S(1)}, u32[]{:S(2)}, u32[]{:S(2)}) collective-permute-start(bf16[1,128,160]{1,2,0:T(8,128)(2,1)S(1)} %get-tuple-element.32), channel_id=1, source_target_pairs={{1,0},{2,1},{3,2},{4,3},{5,4},{6,5},{7,6},{8,7},{9,8},{10,9},{11,1... | collective-permute-start | bytes 122888 | tf_op jit(solution)/shard_map/ppermute | solution.py:19
  217.4 7.1 %collective-permute-start.4 = (bf16[1,128,160]{1,2,0:T(8,128)(2,1)S(1)}, bf16[1,128,160]{1,2,0:T(8,128)(2,1)S(1)}, u32[]{:S(2)}, u32[]{:S(2)}) collective-permute-start(bf16[1,128,160]{1,2,0:T(8,128)(2,1)S(1)} %get-tuple-element.31), channel_id=1, source_target_pairs={{0,1},{1,2},{2,3},{3,4},{4,5},{5,6},{6,7},{7,8},{8,9},{9,10},{10,1... | collective-permute-start | bytes 122888 | tf_op jit(solution)/shard_map/ppermute | solution.py:17
  219.8 4.9 %copy-start.41 = (s32[128]{0:T(128)S(1)}, s32[128]{0:T(128)}, u32[]{:S(2)}) copy-start(s32[128]{0:T(128)} %copy-done.40) | copy-start | bytes 1540
  224.6 1.7 copy-start.39
  229.0 7.1 %copy-start.31 = (s32[1024]{0:T(1024)S(1)}, s32[1024]{0:T(1024)}, u32[]{:S(2)}) copy-start(s32[1024]{0:T(1024)} %copy-done.30) | copy-start | bytes 12292
  231.5 6.9 %collective-permute-start.7 = (bf16[1,128,160]{2,1,0:T(8,128)(2,1)}, bf16[1,128,160]{2,1,0:T(8,128)(2,1)S(1)}, u32[]{:S(2)}, u32[]{:S(2)}) collective-permute-start(bf16[1,128,160]{2,1,0:T(8,128)(2,1)} %bitcast.124), channel_id=1, source_target_pairs={{1,0},{2,1},{3,2},{4,3},{5,4},{6,5},{7,6},{8,7},{9,8},{10,9},{11,1... | collective-permute-start | bytes 122888 | tf_op jit(solution)/shard_map/ppermute | solution.py:19
  233.5 8.3 %collective-permute-start.6 = (bf16[1,128,160]{2,1,0:T(8,128)(2,1)S(1)}, bf16[1,128,160]{2,1,0:T(8,128)(2,1)S(1)}, u32[]{:S(2)}, u32[]{:S(2)}) collective-permute-start(bf16[1,128,160]{2,1,0:T(8,128)(2,1)S(1)} %bitcast.407), channel_id=1, source_target_pairs={{0,1},{1,2},{2,3},{3,4},{4,5},{5,6},{6,7},{7,8},{8,9},{9,10},{10,1... | collective-permute-start | bytes 122888 | tf_op jit(solution)/shard_map/ppermute | solution.py:17
  236.8 1.6 copy-start.10
  236.8 4.9 %copy-start.3 = (f32[768,160]{0,1:T(8,128)S(1)}, f32[768,160]{0,1:T(8,128)}, u32[]{:S(2)}) copy-start(f32[768,160]{0,1:T(8,128)} %get-tuple-element.52) | copy-start | bytes 1474564
  236.8 4.9 %copy-start.4 = (f32[768,160]{0,1:T(8,128)S(1)}, f32[768,160]{0,1:T(8,128)}, u32[]{:S(2)}) copy-start(f32[768,160]{0,1:T(8,128)} %copy.230) | copy-start | bytes 1474564
  236.8 4.9 %copy-start.8 = (bf16[768,128]{1,0:T(8,128)(2,1)S(1)}, bf16[768,128]{1,0:T(8,128)(2,1)}, u32[]{:S(2)}) copy-start(bf16[768,128]{1,0:T(8,128)(2,1)} %param.24) | copy-start | bytes 589828
  236.9 4.9 %copy-start.33 = (f32[768]{0:T(1024)S(1)}, f32[768]{0:T(1024)}, u32[]{:S(2)}) copy-start(f32[768]{0:T(1024)} %param.21) | copy-start | bytes 9220
  241.8 67.8 %copy-start.2 = (f32[768,160]{0,1:T(8,128)S(1)}, f32[768,160]{0,1:T(8,128)}, u32[]{:S(2)}) copy-start(f32[768,160]{0,1:T(8,128)} %param.20) | copy-start | bytes 1474564
